TPU v7x, 256 devices: a whole 4x4x8 slice. The times are simulated.
256 devices in a mesh: feat: 8 (over y, core), dom: 32 (over z, x).
Axes of the slice: x: 4, y: 4, z: 8, core: 2. Of those that a mesh axis runs over, the one named last changes fastest.
Arguments:
- features: bfloat16 [8, 4096, 4096], P(None, 'dom', 'feat'), may hold values from -6 to 6
- w_one: bfloat16 [4096, 1024], P('feat'), may hold values from -0.09375 to 0.09375
- w_two: bfloat16 [1024, 512], replicated, may hold values from -0.25 to 0.25
- neighbor: int32 [8, 4096, 10], P('feat', 'dom'), may hold values from 0 to 383
- degree: int32 [8, 4096], P('feat', 'dom'), may hold values from 1 to 10
- send_rows: int32 [8, 1024, 8], P('feat', 'dom'), may hold values from 0 to 127
- grad_out: bfloat16 [8, 4096, 512], P('feat', 'dom'), may hold values from -6 to 6
Outputs:
- out_two: bfloat16 [8, 4096, 512], P('feat', 'dom')
- grad_one: float32 [4096, 1024], P('feat')
- grad_two: float32 [1024, 512], replicated
All inputs are finite; a program needn't handle non-finite values.
Results may differ from a plain program's by a relative error of at most 0.015.
Values may be sent and summed in bfloat16 or wider, within the bound.
No kernel may reach another device: no remote copies, remote signals or barrier semaphores. Data moves between devices by JAX's collectives and lax.ppermute only.
A program may use at most 64 MiB of HBM per device.

v0:
```python
import math
import jax
import jax.numpy as jnp
from jax import lax
from jax.sharding import PartitionSpec as P


def trade(buffer):
    return lax.all_to_all(buffer, "dom", split_axis=0, concat_axis=0, tiled=True)


def on_device(features, w_one, w_two, neighbor, degree, send_rows, grad_out):
    groups, nodes, cols = features.shape
    width = w_two.shape[1]
    nbrs = neighbor[0]
    degs = degree[0]
    sends = send_rows[0]
    parts = lax.axis_size("dom")
    fan = nbrs.shape[1]
    slots = jnp.arange(fan, dtype=jnp.int32)
    weight = (slots[None, :] < degs[:, None]).astype(jnp.float32) / degs[:, None].astype(
        jnp.float32
    )
    flat = features.reshape(groups * nodes, cols)

    def spread(values):
        boxes = values[sends]
        recv = trade(boxes)
        table = jnp.concatenate([values, recv.reshape(-1, values.shape[1])], axis=0)
        gathered = table[nbrs]
        return jnp.sum(gathered.astype(jnp.float32) * weight[..., None], axis=1)

    def gather_back(grads):
        span = grads.shape[1]
        terms = (weight[..., None] * grads[:, None, :]).reshape(-1, span)
        table = jnp.zeros((nodes + sends.size, span), jnp.float32).at[nbrs.reshape(-1)].add(terms)
        local = table[:nodes]
        outgoing = table[nodes:].astype(jnp.bfloat16).reshape(parts, sends.shape[1], span)
        returned = trade(outgoing)
        home = (
            jnp.zeros((nodes, span), jnp.float32)
            .at[sends.reshape(-1)]
            .add(returned.reshape(-1, span).astype(jnp.float32))
        )
        return local + home

    rows = flat
    proj = lax.psum_scatter(
        jnp.dot(rows, w_one, preferred_element_type=jnp.float32),
        "feat",
        scatter_dimension=0,
        tiled=True,
    )
    p_self = proj[:, :width]
    p_near = proj[:, width:].astype(jnp.bfloat16)
    pre = p_self + spread(p_near)
    hidden = (pre * jax.nn.sigmoid(pre)).astype(jnp.bfloat16)
    agg = spread(hidden).astype(jnp.bfloat16)
    joined = jnp.concatenate([hidden, agg], axis=-1)
    out = jnp.dot(joined, w_two, preferred_element_type=jnp.float32).astype(jnp.bfloat16)
    grads = grad_out[0]
    two_sum = lax.dot_general(
        joined, grads, (((0,), (0,)), ((), ())), preferred_element_type=jnp.float32
    )
    dcat = lax.dot_general(
        grads, w_two, (((1,), (1,)), ((), ())), preferred_element_type=jnp.float32
    )
    d_hidden = dcat[:, :width] + gather_back(dcat[:, width:])
    sig = jax.nn.sigmoid(pre)
    d_pre = d_hidden * sig * (1.0 + pre * (1.0 - sig))
    d_near = gather_back(d_pre)
    d_proj = jnp.concatenate([d_pre, d_near], axis=-1).astype(jnp.bfloat16)
    rows = flat
    one_sum = lax.dot_general(
        rows,
        lax.all_gather(d_proj, "feat", axis=0, tiled=True),
        (((0,), (0,)), ((), ())),
        preferred_element_type=jnp.float32,
    )
    one_sum = lax.psum(one_sum.astype(jnp.bfloat16), "dom").astype(jnp.float32)
    two_sum = lax.psum(two_sum, ("feat", "dom"))
    scale = 1.0 / math.sqrt(groups * nodes * parts)
    return (out[None], one_sum * scale, two_sum * scale)


def solution(mesh):
    in_specs = (
        P(None, "dom", "feat"),
        P("feat", None),
        P(),
        P("feat", "dom", None),
        P("feat", "dom"),
        P("feat", "dom", None),
        P("feat", "dom", None),
    )
    out_specs = (P("feat", "dom", None), P("feat", None), P())
    return jax.shard_map(
        on_device, mesh=mesh, in_specs=in_specs, out_specs=out_specs, check_vma=False
    )
```

profile of v0, /device:TPU:8, one launch (start us, length us, event | category | flops | bytes accessed | tf_op | source)
XLA Modules:
  0.0 582.7 jit_solution(4482622993260259353)
XLA Ops:
  7.2 1.2 copy-done
  8.4 4.4 fusion.26
  14.5 2.5 mul.73
  17.0 4.5 mul.74
  21.9 13.1 %scatter_custom_fusion = f32[384,512]{1,0:T(8,128)S(1)} fusion(s32[1280]{0:T(1024)S(1)} %fusion.22, f32[1280,512]{1,0:T(8,128)} %mul.74, f32[1280]{0:T(1024)S(1)} %div.23, f32[]{:T(128)} %constant.9.clone.1), kind=kCustom, calls=%fused_computation.12 | custom fusion | flops 1310720 | bytes 3416068 | tf_op jit(solution)/shard_map/scatter-add | solution.py:36
  35.7 11.3 %all-to-all-start.2 = ((bf16[32,8,512]{2,1,0:T(8,128)(2,1)}), bf16[32,8,512]{2,1,0:T(8,128)(2,1)S(1)}, u32[]{:S(2)}, u32[]{:S(2)}) async-start(bf16[32,8,512]{2,1,0:T(8,128)(2,1)} %fusion.14), calls=%async_computation.3 | async-start | bytes 524288 | tf_op jit(solution)/shard_map/all_to_all | solution.py:9
  47.5 5.2 reduce-scatter.2.cloned.1.call-done
  53.7 1.9 gather_fusion
  55.5 4.2 all-to-all-done.2
  59.7 5.7 all-to-all-start
  65.6 2.4 scatter_custom_fusion.1
  68.0 10.6 %all-to-all-done = bf16[32,8,512]{2,1,0:T(8,128)(2,1)S(1)} async-done(((bf16[32,8,512]{2,1,0:T(8,128)(2,1)}), bf16[32,8,512]{2,1,0:T(8,128)(2,1)S(1)}, u32[]{:S(2)}, u32[]{:S(2)}) %all-to-all-start) | async-done | bytes 262176 | tf_op jit(solution)/shard_map/all_to_all | solution.py:9
  78.7 4.1 gather_fusion.1
  82.8 2.1 reshape.277
  84.9 3.2 multiply_reduce_fusion.1
  88.3 2.5 mul.79
  90.8 4.5 mul.80
  95.3 13.1 %scatter_custom_fusion.2 = f32[384,512]{1,0:T(8,128)S(1)} fusion(s32[1280]{0:T(1024)S(1)} %fusion.22, f32[1280,512]{1,0:T(8,128)} %mul.80, f32[1280]{0:T(1024)S(1)} %div.23, f32[]{:T(128)} %constant.9.clone.1), kind=kCustom, calls=%fused_computation.10 | custom fusion | flops 1310720 | bytes 3416068 | tf_op jit(solution)/shard_map/scatter-add | solution.py:36
  109.1 3.9 all-to-all-start.3
  113.0 12.2 %all-to-all-done.3 = bf16[32,8,512]{2,1,0:T(8,128)(2,1)S(1)} async-done(((bf16[32,8,512]{2,1,0:T(8,128)(2,1)}), bf16[32,8,512]{2,1,0:T(8,128)(2,1)S(1)}, u32[]{:S(2)}, u32[]{:S(2)}) %all-to-all-start.3) | async-done | bytes 262176 | tf_op jit(solution)/shard_map/all_to_all | solution.py:9
  125.3 2.2 scatter_custom_fusion.3
  129.5 15.7 %all_to_all.20 = bf16[32,8,512]{2,1,0:T(8,128)(2,1)S(1)} all-to-all(bf16[32,8,512]{2,1,0:T(8,128)(2,1)S(1)} %bitcast.50), channel_id=1, replica_groups=mesh['feat'=8,'dom'=32] {'dom'}, dimensions={0} | all-to-all | bytes 524288 | tf_op jit(solution)/shard_map/all_to_all | solution.py:9
  145.3 4.1 gather_fusion.3
  149.4 2.1 reshape.278
  151.6 3.2 multiply_reduce_fusion
  154.8 1.8 fusion.18
  156.7 3.9 fusion.4
  161.6 259.2 %all-reduce.5.cloned.1.call-done = f32[1024,512]{1,0:T(8,128)} async-done(((f32[1024,512]{1,0:T(8,128)}), f32[1024,512]{1,0:T(8,128)}) %all-reduce.5.cloned.1.call-update) | async-done | bytes 2097168 | tf_op jit(solution)/shard_map/psum | solution.py:81
  420.8 3.2 broadcast_multiply_fusion
  423.9 148.9 %all-reduce.3.cloned.1.call-done = bf16[512,1024]{0,1:T(8,128)(2,1)} async-done(((bf16[512,1024]{0,1:T(8,128)(2,1)}), bf16[512,1024]{0,1:T(8,128)(2,1)}) %all-reduce.3.cloned.1.call-update) | async-done | bytes 1048592 | tf_op jit(solution)/shard_map/psum | solution.py:80
  572.8 1.5 convert_multiply_fusion
  574.4 1.8 copy.15
  (57 shorter events, 8.4 us)
Async XLA Ops:
  7.2 1.2 copy-start
  7.2 45.5 %reduce-scatter.2.cloned.1.call-start = ((), (), s32[]{:S(2)}) async-start(), calls=%async_computation.5 | async-start | bytes 4718592 | tf_op jit(solution)/shard_map/reduce_scatter | solution.py:48
  12.8 0.7 copy-start.6
  12.8 1.2 copy-start.1
  12.8 1.2 copy-start.3
  17.0 4.5 copy-start.8
  21.6 25.4 %copy-start.7 = (s32[1,32,8]{1,2,0:T(8,128)S(1)}, s32[1,32,8]{1,2,0:T(8,128)}, u32[]{:S(2)}) copy-start(s32[1,32,8]{1,2,0:T(8,128)} %param.12) | copy-start | bytes 3076
  35.7 24.0 %all-to-all-start.2 = ((bf16[32,8,512]{2,1,0:T(8,128)(2,1)}), bf16[32,8,512]{2,1,0:T(8,128)(2,1)S(1)}, u32[]{:S(2)}, u32[]{:S(2)}) async-start(bf16[32,8,512]{2,1,0:T(8,128)(2,1)} %fusion.14), calls=%async_computation.3 | async-start | bytes 524288 | tf_op jit(solution)/shard_map/all_to_all | solution.py:9
  59.7 18.9 %all-to-all-start = ((bf16[32,8,512]{2,1,0:T(8,128)(2,1)}), bf16[32,8,512]{2,1,0:T(8,128)(2,1)S(1)}, u32[]{:S(2)}, u32[]{:S(2)}) async-start(bf16[32,8,512]{2,1,0:T(8,128)(2,1)} %bitcast.2), calls=%async_computation.1 | async-start | bytes 524288 | tf_op jit(solution)/shard_map/all_to_all | solution.py:9
  84.9 3.3 copy-start.5
  109.1 16.2 %all-to-all-start.3 = ((bf16[32,8,512]{2,1,0:T(8,128)(2,1)}), bf16[32,8,512]{2,1,0:T(8,128)(2,1)S(1)}, u32[]{:S(2)}, u32[]{:S(2)}) async-start(bf16[32,8,512]{2,1,0:T(8,128)(2,1)} %fusion.15), calls=%async_computation.4 | async-start | bytes 524288 | tf_op jit(solution)/shard_map/all_to_all | solution.py:9
  113.0 43.7 %all-gather.2.cloned.1.call-start = ((), (), s32[]{:S(2)}) async-start(), calls=%async_computation.6 | async-start | bytes 2359296 | tf_op jit(solution)/shard_map/all_gather | solution.py:76
  128.3 292.5 %all-reduce.5.cloned.1.call-start = ((), (), s32[]{:S(2)}) async-start(), calls=%async_computation.8 | async-start | bytes 4194304 | tf_op jit(solution)/shard_map/psum | solution.py:81
  151.6 3.2 copy-start.4
  156.6 4.0 copy-start.2
  156.6 416.2 %all-reduce.3.cloned.1.call-start = ((), (), s32[]{:S(2)}) async-start(), calls=%async_computation.7 | async-start | bytes 2097152 | tf_op jit(solution)/shard_map/psum | solution.py:80
Sparse Core Ops, SparseCore 0:
  12.9 39.6 reduce-scatter.1
  128.4 23.6 all-gather.1
  158.1 262.6 all-reduce.4
  424.7 148.1 all-reduce.2
where the time goes:
time: 583 us
  waiting for transfers between devices  440 us (75%)
  other arithmetic  43.1 us (7%)
  local copies, waits for them, and re-layouts  36.9 us (6%)
  starting transfers between devices  21 us (4%)
  blocking collectives  15.7 us (3%)
  between operations  14.1 us (2%)
  matrix products  11.5 us (2%)
    psum x1, waiting for transfers between devices, on_device(): two_sum = lax.psum(two_sum, ('feat', 'dom'))  259 us
    psum x1, waiting for transfers between devices, on_device(): one_sum = lax.psum(one_sum.astype(jnp.bfloat16), 'dom').astype(jnp.float32)  149 us
    all_to_all x3, waiting for transfers between devices, trade(): lax.all_to_all(buffer, 'dom', split_axis=0, concat_axis=0, tiled=True)  27 us
    scatter-add x2, other arithmetic, gather_back(): jnp.zeros((nodes + sends.size, span), jnp.float32).at[nbrs.reshape(-1)]  26.1 us
    all_to_all x3, starting transfers between devices, trade(): lax.all_to_all(buffer, 'dom', split_axis=0, concat_axis=0, tiled=True)  20.8 us
    all_to_all x1, blocking collectives, trade(): lax.all_to_all(buffer, 'dom', split_axis=0, concat_axis=0, tiled=True)  15.7 us
    mul x4, local copies, waits for them, and re-layouts, gather_back(): terms = (weight[..., None] * grads[:, None, :]).reshape(-1, span)  14 us
  transfers between devices with their start and end apart: 7, of which 6 were waited for; matrix products, arithmetic and copies ran while one was open for 8% of the time, Pallas kernels for 0%

commit v1 on v0

--- a/solution.py
+++ b/solution.py
@@ -78,7 +78,8 @@
         preferred_element_type=jnp.float32,
     )
     one_sum = lax.psum(one_sum.astype(jnp.bfloat16), "dom").astype(jnp.float32)
-    two_sum = lax.psum(two_sum, ("feat", "dom"))
+    for mesh_axis in ("feat", "dom"):
+        two_sum = lax.psum(two_sum, mesh_axis)
     scale = 1.0 / math.sqrt(groups * nodes * parts)
     return (out[None], one_sum * scale, two_sum * scale)
 

time: 583 us -> 534 us (0.916)
  waiting for transfers between devices: 440 us -> 390 us
    psum x1 -> x2, waiting for transfers between devices: 259 us -> 180 us  [on_device(): two_sum = lax.psum(two_sum, mesh_axis)]
    all_gather x1, waiting for transfers between devices: 0.02 us -> 31.2 us  [on_device(): lax.all_gather(d_proj, 'feat', axis=0, tiled=True)]
  transfers between devices with their start and end apart: 7 -> 8, of which waited for: 6 -> 8; matrix products, arithmetic and copies ran while one was open for 8% -> 11% of each run, Pallas kernels for 0% -> 0%
where the time goes in v1:
time: 534 us
  waiting for transfers between devices  390 us (73%)
  other arithmetic  43.8 us (8%)
  local copies, waits for them, and re-layouts  36.8 us (7%)
  starting transfers between devices  21 us (4%)
  blocking collectives  16 us (3%)
  between operations  14.1 us (3%)
  matrix products  11.5 us (2%)
    psum x2, waiting for transfers between devices, on_device(): two_sum = lax.psum(two_sum, mesh_axis)  180 us
    psum x1, waiting for transfers between devices, on_device(): one_sum = lax.psum(one_sum.astype(jnp.bfloat16), 'dom').astype(jnp.float32)  147 us
    all_gather x1, waiting for transfers between devices, on_device(): lax.all_gather(d_proj, 'feat', axis=0, tiled=True)  31.2 us
    all_to_all x3, waiting for transfers between devices, trade(): lax.all_to_all(buffer, 'dom', split_axis=0, concat_axis=0, tiled=True)  26.6 us
    scatter-add x2, other arithmetic, gather_back(): jnp.zeros((nodes + sends.size, span), jnp.float32).at[nbrs.reshape(-1)]  26.2 us
    all_to_all x3, starting transfers between devices, trade(): lax.all_to_all(buffer, 'dom', split_axis=0, concat_axis=0, tiled=True)  20.8 us
    all_to_all x1, blocking collectives, trade(): lax.all_to_all(buffer, 'dom', split_axis=0, concat_axis=0, tiled=True)  16 us
    mul x4, local copies, waits for them, and re-layouts, gather_back(): terms = (weight[..., None] * grads[:, None, :]).reshape(-1, span)  14 us
  transfers between devices with their start and end apart: 8, of which 8 were waited for; matrix products, arithmetic and copies ran while one was open for 11% of the time, Pallas kernels for 0%

profile of v1, /device:TPU:8, one launch (start us, length us, event | category | flops | bytes accessed | tf_op | source)
XLA Modules:
  0.0 533.6 jit_solution(9362710205576431516)
XLA Ops:
  8.4 4.4 fusion.26
  14.5 2.5 mul.73
  17.0 4.5 mul.74
  21.9 13.1 %scatter_custom_fusion = f32[384,512]{1,0:T(8,128)S(1)} fusion(s32[1280]{0:T(1024)S(1)} %fusion.22, f32[1280,512]{1,0:T(8,128)} %mul.74, f32[1280]{0:T(1024)S(1)} %div.23, f32[]{:T(128)} %constant.9.clone.1), kind=kCustom, calls=%fused_computation.12 | custom fusion | flops 1310720 | bytes 3416068 | tf_op jit(solution)/shard_map/scatter-add | solution.py:36
  35.7 11.3 %all-to-all-start.2 = ((bf16[32,8,512]{2,1,0:T(8,128)(2,1)}), bf16[32,8,512]{2,1,0:T(8,128)(2,1)S(1)}, u32[]{:S(2)}, u32[]{:S(2)}) async-start(bf16[32,8,512]{2,1,0:T(8,128)(2,1)} %fusion.14), calls=%async_computation.3 | async-start | bytes 524288 | tf_op jit(solution)/shard_map/all_to_all | solution.py:9
  47.5 5.2 reduce-scatter.2.cloned.1.call-done
  53.7 1.9 gather_fusion
  55.5 4.2 all-to-all-done.2
  59.7 5.7 %all-to-all-start = ((bf16[32,8,512]{2,1,0:T(8,128)(2,1)}), bf16[32,8,512]{2,1,0:T(8,128)(2,1)S(1)}, u32[]{:S(2)}, u32[]{:S(2)}) async-start(bf16[32,8,512]{2,1,0:T(8,128)(2,1)} %bitcast.2), calls=%async_computation.1 | async-start | bytes 524288 | tf_op jit(solution)/shard_map/all_to_all | solution.py:9
  65.6 2.4 scatter_custom_fusion.1
  68.1 10.5 %all-to-all-done = bf16[32,8,512]{2,1,0:T(8,128)(2,1)S(1)} async-done(((bf16[32,8,512]{2,1,0:T(8,128)(2,1)}), bf16[32,8,512]{2,1,0:T(8,128)(2,1)S(1)}, u32[]{:S(2)}, u32[]{:S(2)}) %all-to-all-start) | async-done | bytes 262176 | tf_op jit(solution)/shard_map/all_to_all | solution.py:9
  78.7 4.1 gather_fusion.1
  82.8 2.1 reshape.277
  84.9 3.2 multiply_reduce_fusion.1
  90.1 16.0 %all_to_all.20 = bf16[32,8,512]{2,1,0:T(8,128)(2,1)S(1)} all-to-all(bf16[32,8,512]{2,1,0:T(8,128)(2,1)S(1)} %bitcast.50), channel_id=1, replica_groups=mesh['feat'=8,'dom'=32] {'dom'}, dimensions={0} | all-to-all | bytes 524288 | tf_op jit(solution)/shard_map/all_to_all | solution.py:9
  106.1 4.1 gather_fusion.3
  110.2 2.1 reshape.278
  112.3 3.2 multiply_reduce_fusion
  115.6 1.8 fusion.18
  117.4 2.5 mul.79
  119.8 4.5 mul.80
  124.4 13.2 %scatter_custom_fusion.2 = f32[384,512]{1,0:T(8,128)S(1)} fusion(s32[1280]{0:T(1024)S(1)} %fusion.22, f32[1280,512]{1,0:T(8,128)} %mul.80, f32[1280]{0:T(1024)S(1)} %div.23, f32[]{:T(128)} %constant.9.clone.1), kind=kCustom, calls=%fused_computation.10 | custom fusion | flops 1310720 | bytes 3416068 | tf_op jit(solution)/shard_map/scatter-add | solution.py:36
  138.3 3.9 all-to-all-start.3
  142.2 11.9 %all-to-all-done.3 = bf16[32,8,512]{2,1,0:T(8,128)(2,1)S(1)} async-done(((bf16[32,8,512]{2,1,0:T(8,128)(2,1)}), bf16[32,8,512]{2,1,0:T(8,128)(2,1)S(1)}, u32[]{:S(2)}, u32[]{:S(2)}) %all-to-all-start.3) | async-done | bytes 262176 | tf_op jit(solution)/shard_map/all_to_all | solution.py:9
  154.1 2.2 scatter_custom_fusion.3
  157.2 25.7 %all-reduce.6.cloned.1.call-done = f32[1024,512]{1,0:T(8,128)} async-done(((f32[1024,512]{1,0:T(8,128)}), f32[1024,512]{1,0:T(8,128)}) %all-reduce.6.cloned.1.call-update) | async-done | bytes 2097168 | tf_op jit(solution)/shard_map/psum | solution.py:82
  183.0 31.2 %all-gather.2.cloned.1.call-done = bf16[1024,1024]{1,0:T(8,128)(2,1)} async-done(((bf16[128,1024]{1,0:T(8,128)(2,1)}), bf16[1024,1024]{1,0:T(8,128)(2,1)}) %all-gather.2.cloned.1.call-update) | async-done | bytes 2097168 | tf_op jit(solution)/shard_map/all_gather | solution.py:76
  214.2 3.8 fusion.4
  219.0 154.2 %all-reduce.8.cloned.1.call-done = f32[1024,512]{1,0:T(8,128)} async-done(((f32[1024,512]{1,0:T(8,128)}), f32[1024,512]{1,0:T(8,128)}) %all-reduce.8.cloned.1.call-update) | async-done | bytes 2097168 | tf_op jit(solution)/shard_map/psum | solution.py:82
  373.2 3.2 broadcast_multiply_fusion
  376.4 147.3 %all-reduce.4.cloned.1.call-done = bf16[512,1024]{0,1:T(8,128)(2,1)} async-done(((bf16[512,1024]{0,1:T(8,128)(2,1)}), bf16[512,1024]{0,1:T(8,128)(2,1)}) %all-reduce.4.cloned.1.call-update) | async-done | bytes 1048592 | tf_op jit(solution)/shard_map/psum | solution.py:80
  525.2 1.8 copy.15
  (62 shorter events, 11.8 us)
Async XLA Ops:
  7.2 1.2 copy-start
  7.2 45.5 %reduce-scatter.2.cloned.1.call-start = ((), (), s32[]{:S(2)}) async-start(), calls=%async_computation.5 | async-start | bytes 4718592 | tf_op jit(solution)/shard_map/reduce_scatter | solution.py:48
  12.8 0.7 copy-start.7
  12.8 1.2 copy-start.1
  12.8 1.2 copy-start.4
  17.0 4.5 copy-start.9
  21.6 25.4 %copy-start.8 = (s32[1,32,8]{1,2,0:T(8,128)S(1)}, s32[1,32,8]{1,2,0:T(8,128)}, u32[]{:S(2)}) copy-start(s32[1,32,8]{1,2,0:T(8,128)} %param.12) | copy-start | bytes 3076
  35.7 24.0 %all-to-all-start.2 = ((bf16[32,8,512]{2,1,0:T(8,128)(2,1)}), bf16[32,8,512]{2,1,0:T(8,128)(2,1)S(1)}, u32[]{:S(2)}, u32[]{:S(2)}) async-start(bf16[32,8,512]{2,1,0:T(8,128)(2,1)} %fusion.14), calls=%async_computation.3 | async-start | bytes 524288 | tf_op jit(solution)/shard_map/all_to_all | solution.py:9
  59.7 18.9 %all-to-all-start = ((bf16[32,8,512]{2,1,0:T(8,128)(2,1)}), bf16[32,8,512]{2,1,0:T(8,128)(2,1)S(1)}, u32[]{:S(2)}, u32[]{:S(2)}) async-start(bf16[32,8,512]{2,1,0:T(8,128)(2,1)} %bitcast.2), calls=%async_computation.1 | async-start | bytes 524288 | tf_op jit(solution)/shard_map/all_to_all | solution.py:9
  65.4 117.5 %all-reduce.6.cloned.1.call-start = ((), (), s32[]{:S(2)}) async-start(), calls=%async_computation.8 | async-start | bytes 4194304 | tf_op jit(solution)/shard_map/psum | solution.py:82
  84.9 3.3 copy-start.6
  112.3 3.2 copy-start.5
  124.3 32.0 %copy-start.3 = (bf16[128,512]{1,0:T(8,128)(2,1)S(1)}, bf16[128,512]{1,0:T(8,128)(2,1)}, u32[]{:S(2)}) copy-start(bf16[128,512]{1,0:T(8,128)(2,1)} %get-tuple-element.9) | copy-start | bytes 393220
  138.3 15.9 %all-to-all-start.3 = ((bf16[32,8,512]{2,1,0:T(8,128)(2,1)}), bf16[32,8,512]{2,1,0:T(8,128)(2,1)S(1)}, u32[]{:S(2)}, u32[]{:S(2)}) async-start(bf16[32,8,512]{2,1,0:T(8,128)(2,1)} %fusion.15), calls=%async_computation.4 | async-start | bytes 524288 | tf_op jit(solution)/shard_map/all_to_all | solution.py:9
  142.1 72.0 %all-gather.2.cloned.1.call-start = ((), (), s32[]{:S(2)}) async-start(), calls=%async_computation.6 | async-start | bytes 2359296 | tf_op jit(solution)/shard_map/all_gather | solution.py:76
  157.2 216.1 %all-reduce.8.cloned.1.call-start = ((), (), s32[]{:S(2)}) async-start(), calls=%async_computation.9 | async-start | bytes 4194304 | tf_op jit(solution)/shard_map/psum | solution.py:82
  182.9 35.1 %copy-start.2 = (bf16[1024,512]{1,0:T(8,128)(2,1)S(1)}, bf16[1024,512]{1,0:T(8,128)(2,1)}, u32[]{:S(2)}) copy-start(bf16[1024,512]{1,0:T(8,128)(2,1)} %param.9) | copy-start | bytes 3145732
  182.9 340.7 %all-reduce.4.cloned.1.call-start = ((), (), s32[]{:S(2)}) async-start(), calls=%async_computation.7 | async-start | bytes 2097152 | tf_op jit(solution)/shard_map/psum | solution.py:80
Sparse Core Ops, SparseCore 0:
  12.9 39.6 reduce-scatter.1
  117.5 65.3 all-reduce.5
  185.3 28.7 all-gather.1
  217.5 155.6 all-reduce.7
  377.5 146.1 all-reduce.3
